TPU v7x, 32 devices: a whole 2x2x4 slice. The times are simulated.
32 devices in a mesh: expert: 8 (over z, x), tensor: 4 (over y, core).
Axes of the slice: x: 2, y: 2, z: 4, core: 2. Of those that a mesh axis runs over, the one named last changes fastest.
Arguments:
- tokens: bfloat16 [512, 8192], P('expert', 'tensor'), may hold values from -6 to 6
- frozen_gate_weight: bfloat16 [8192, 28672], P('tensor', 'expert'), may hold values from -0.0625 to 0.0625
- frozen_up_weight: bfloat16 [8192, 28672], P('tensor', 'expert'), may hold values from -0.0625 to 0.0625
- frozen_down_weight: bfloat16 [28672, 8192], P('expert', 'tensor'), may hold values from -0.03125 to 0.03125
- adapter_down_weight: bfloat16 [32, 8192, 128], P('expert', 'tensor'), may hold values from -0.0625 to 0.0625
- adapter_up_weight: bfloat16 [32, 128, 8192], P('expert', None, 'tensor'), may hold values from -0.0625 to 0.0625
- routes: int32 [512, 2], P('expert'), may hold values from 0 to 31, all different within a row; in each aligned block of 64 rows (0 to 63, 64 to 127, ...) at most 8 rows name the same one
- route_gate_weights: float32 [512, 2], P('expert'), may hold values from 0.1 to 1
- output_gradient: bfloat16 [512, 8192], P('expert', 'tensor'), may hold values from -6 to 6
Outputs:
- ffn_out: bfloat16 [512, 8192], P('expert', 'tensor')
- grad_down: bfloat16 [32, 8192, 128], P('expert', 'tensor')
- grad_up: bfloat16 [32, 128, 8192], P('expert', None, 'tensor')
Inputs may be any that keep to these rules, and one draw needn't show every extreme that they name: `routes`: the two experts of a token differ. Among the 64 rows of one index of expert no expert is named more than 8 times, and in some such rows one expert is named exactly 8 times.
All inputs are finite; a program needn't handle non-finite values.
Results may differ from a plain program's by a relative error of at most 0.025.
Values may be sent and summed in bfloat16 or wider, within the bound.
A program may use at most 128 MiB of HBM per device.

v0:
```python
import jax
import jax.numpy as jnp
from jax import lax
from jax.sharding import PartitionSpec as P


def activate(summed, hidden_width):
    gate_part = summed[:, :hidden_width]
    up_part = summed[:, hidden_width:]
    return (jax.nn.silu(gate_part) * up_part).astype(jnp.bfloat16)


def per_device(
    tokens,
    frozen_gate_weight,
    frozen_up_weight,
    frozen_down_weight,
    adapter_down_weight,
    adapter_up_weight,
    routes,
    route_gate_weights,
    output_gradient,
):
    n_expert = lax.axis_size("expert")
    tok_count, width_part = tokens.shape
    hidden_width = frozen_gate_weight.shape[1]
    expert_resident = adapter_down_weight.shape[0]
    all_experts = expert_resident * n_expert
    most_slots = max(2, 4 * tok_count // all_experts)
    slot_total = all_experts * most_slots
    per_peer = expert_resident * most_slots
    shard_rows = lax.all_gather(tokens, "expert", axis=0, tiled=True)
    gate_part = jnp.dot(shard_rows, frozen_gate_weight, preferred_element_type=jnp.float32)
    up_part = jnp.dot(shard_rows, frozen_up_weight, preferred_element_type=jnp.float32)
    partial_value = jnp.concatenate([gate_part, up_part], axis=1)
    summed = lax.psum_scatter(
        partial_value.astype(jnp.bfloat16), "tensor", scatter_dimension=0, tiled=True
    ).astype(jnp.float32)
    hidden_all = lax.all_gather(activate(summed, hidden_width), "tensor", axis=0, tiled=True)
    base_out = lax.psum_scatter(
        jnp.dot(hidden_all, frozen_down_weight, preferred_element_type=jnp.float32).astype(
            jnp.bfloat16
        ),
        "expert",
        scatter_dimension=0,
        tiled=True,
    ).astype(jnp.float32)
    route_ids = routes.reshape(-1)
    pair_count = route_ids.shape[0]
    expert_range = jnp.arange(all_experts, dtype=jnp.int32)
    member = (route_ids[:, None] == expert_range[None, :]).astype(jnp.bfloat16)
    pair_range = jnp.arange(pair_count, dtype=jnp.int32)
    before = (pair_range[:, None] > pair_range[None, :]).astype(jnp.bfloat16)
    earlier = jnp.dot(before, member, preferred_element_type=jnp.float32)
    within = jnp.sum(earlier * member.astype(jnp.float32), axis=1).astype(jnp.int32)
    target = route_ids * most_slots + within
    slot_range = jnp.arange(slot_total, dtype=jnp.int32)
    select = (slot_range[:, None] == target[None, :]).astype(jnp.bfloat16)
    to_slots = jnp.sum(select.reshape(slot_total, tok_count, 2), axis=2)
    send_inputs = jnp.dot(to_slots, tokens, preferred_element_type=jnp.float32).astype(jnp.bfloat16)
    send_inputs = send_inputs.reshape(n_expert, per_peer, width_part)
    scaled = (
        route_gate_weights[:, :, None] * output_gradient[:, None, :].astype(jnp.float32)
    ).astype(jnp.bfloat16)
    scaled = scaled.reshape(pair_count, width_part)
    send_grads = jnp.dot(select, scaled, preferred_element_type=jnp.float32).astype(jnp.bfloat16)
    send_grads = send_grads.reshape(n_expert, per_peer, width_part)
    incoming_input_rows = lax.all_to_all(
        send_inputs, "expert", split_axis=0, concat_axis=0, tiled=True
    )
    incoming_input_rows = incoming_input_rows.reshape(
        n_expert, expert_resident, most_slots, width_part
    )
    low_sum = lax.psum(
        jnp.einsum(
            "bcwk,cko->cbwo",
            incoming_input_rows,
            adapter_down_weight,
            preferred_element_type=jnp.float32,
        ).astype(jnp.bfloat16),
        "tensor",
    )
    expert_out = jnp.einsum(
        "lugx,lxo->ulgo", low_sum, adapter_up_weight, preferred_element_type=jnp.float32
    ).astype(jnp.bfloat16)
    returned = lax.all_to_all(
        expert_out.reshape(n_expert, per_peer, width_part),
        "expert",
        split_axis=0,
        concat_axis=0,
        tiled=True,
    )
    per_pair = jnp.dot(
        select.T, returned.reshape(slot_total, width_part), preferred_element_type=jnp.float32
    )
    per_pair = per_pair.reshape(tok_count, 2, width_part)
    adapter_sum = (
        route_gate_weights[:, 0:1] * per_pair[:, 0, :]
        + route_gate_weights[:, 1:2] * per_pair[:, 1, :]
    )
    ffn_out = (base_out + adapter_sum).astype(jnp.bfloat16)
    incoming_gradients = lax.all_to_all(
        send_grads, "expert", split_axis=0, concat_axis=0, tiled=True
    )
    incoming_gradients = incoming_gradients.reshape(
        n_expert, expert_resident, most_slots, width_part
    )
    back_sum = lax.psum(
        jnp.einsum(
            "nhpf,hxf->hnpx",
            incoming_gradients,
            adapter_up_weight,
            preferred_element_type=jnp.float32,
        ).astype(jnp.bfloat16),
        "tensor",
    )
    grad_up = jnp.einsum(
        "jsmr,sjmd->jrd", low_sum, incoming_gradients, preferred_element_type=jnp.float32
    ).astype(jnp.bfloat16)
    grad_down = jnp.einsum(
        "sjmd,jsmr->jdr", incoming_input_rows, back_sum, preferred_element_type=jnp.float32
    ).astype(jnp.bfloat16)
    return (ffn_out, grad_down, grad_up)


def solution(mesh):
    placed = (
        P("expert", "tensor"),
        P("tensor", "expert"),
        P("tensor", "expert"),
        P("expert", "tensor"),
        P("expert", "tensor", None),
        P("expert", None, "tensor"),
        P("expert", None),
        P("expert", None),
        P("expert", "tensor"),
    )
    return jax.shard_map(
        per_device,
        mesh=mesh,
        in_specs=placed,
        out_specs=(P("expert", "tensor"), P("expert", "tensor", None), P("expert", None, "tensor")),
        check_vma=False,
    )
```

profile of v0, /device:TPU:0, one launch (start us, length us, event | category | flops | bytes accessed | tf_op | source)
XLA Modules:
  0.0 356.5 jit_solution(9830163328550035932)
XLA Ops:
  7.2 0.0 all-gather.3.cloned.1.call-start
  7.2 0.7 all-gather.3.cloned.1.call-update
  7.9 0.0 reduce-scatter.3.cloned.1.call-start
  8.0 54.0 %all-gather.3.cloned.1.call-done = bf16[512,2048]{1,0:T(8,128)(2,1)} async-done(((bf16[64,2048]{1,0:T(8,128)(2,1)}), bf16[512,2048]{1,0:T(8,128)(2,1)}) %all-gather.3.cloned.1.call-update) | async-done | bytes 2097168 | tf_op jit(solution)/shard_map/all_gather | solution.py:32
  62.0 14.9 %convolution_convert_fusion = bf16[512,3584]{1,0:T(8,128)(2,1)} fusion(bf16[512,2048]{1,0:T(8,128)(2,1)} %all-gather.3.cloned.1.call-done, bf16[2048,3584]{1,0:T(8,128)(2,1)} %param.11), kind=kOutput, calls=%fused_computation.1 | convolution fusion | flops 7518027776 | bytes 20447232 | tf_op jit(solution)/shard_map/dot_general | solution.py:34
  76.9 12.4 %convolution_convert_fusion.1 = bf16[512,3584]{1,0:T(8,128)(2,1)} fusion(bf16[512,2048]{1,0:T(8,128)(2,1)S(1)} %copy-done.6, bf16[2048,3584]{1,0:T(8,128)(2,1)} %param.10), kind=kOutput, calls=%fused_computation.2 | convolution fusion | flops 7518027776 | bytes 20447232 | tf_op jit(solution)/shard_map/dot_general | solution.py:33
  89.3 6.9 %pad_maximum_fusion = bf16[512,7168]{1,0:T(8,128)(2,1)} fusion(bf16[512,3584]{1,0:T(8,128)(2,1)} %convolution_convert_fusion, bf16[512,3584]{1,0:T(8,128)(2,1)} %convolution_convert_fusion.1), kind=kLoop, calls=%fused_computation | loop fusion | flops 14680064 | bytes 14680064 | tf_op jit(solution)/shard_map/concatenate | solution.py:35
  96.1 0.0 reduce-scatter.3.cloned.1.call-update
  96.2 0.0 all-gather.5.cloned.1.call-start
  96.2 64.6 %reduce-scatter.3.cloned.1.call-done = bf16[128,7168]{1,0:T(8,128)(2,1)} async-done(((bf16[512,7168]{1,0:T(8,128)(2,1)}), bf16[128,7168]{1,0:T(8,128)(2,1)}) %reduce-scatter.3.cloned.1.call-update) | async-done | bytes 1835024 | tf_op jit(solution)/shard_map/reduce_scatter | solution.py:36
  160.8 1.9 convert_element_type.72
  162.7 1.5 fusion.6
  164.2 0.1 copy.40
  164.3 0.1 reshape.81
  164.4 0.5 mul.78
  164.9 1.7 mul.79
  166.6 0.1 copy.45
  166.7 0.1 mul.76
  166.9 0.2 fusion.13
  167.1 2.7 convolution_convert_fusion.3
  169.8 5.5 %all-to-all-start.2 = ((bf16[8,32,2048]{2,1,0:T(8,128)(2,1)}), bf16[8,32,2048]{2,1,0:T(8,128)(2,1)S(1)}, u32[]{:S(2)}, u32[]{:S(2)}) async-start(bf16[8,32,2048]{2,1,0:T(8,128)(2,1)} %bitcast.77), calls=%async_computation.4 | async-start | bytes 2097152 | tf_op jit(solution)/shard_map/all_to_all | solution.py:102
  175.3 0.1 convert_element_type.79
  175.5 0.1 copy.41
  175.5 0.1 fusion.25
  175.7 1.4 convolution_convert_fusion.5
  177.1 23.9 %all-to-all-done.2 = bf16[8,32,2048]{2,1,0:T(8,128)(2,1)S(1)} async-done(((bf16[8,32,2048]{2,1,0:T(8,128)(2,1)}), bf16[8,32,2048]{2,1,0:T(8,128)(2,1)S(1)}, u32[]{:S(2)}, u32[]{:S(2)}) %all-to-all-start.2) | async-done | bytes 1048608 | tf_op jit(solution)/shard_map/all_to_all | solution.py:102
  201.0 4.3 %all-to-all-start = ((bf16[8,32,2048]{2,1,0:T(8,128)(2,1)}), bf16[8,32,2048]{2,1,0:T(8,128)(2,1)}, u32[]{:S(2)}, u32[]{:S(2)}) async-start(bf16[8,32,2048]{2,1,0:T(8,128)(2,1)} %bitcast.76), calls=%async_computation.2 | async-start | bytes 2097152 | tf_op jit(solution)/shard_map/all_to_all | solution.py:68
  205.2 0.0 all-reduce.3.cloned.1.call-start
  205.3 0.6 copy.46
  205.9 1.5 fusion.7
  207.4 23.4 %all-to-all-done = bf16[8,32,2048]{2,1,0:T(8,128)(2,1)} async-done(((bf16[8,32,2048]{2,1,0:T(8,128)(2,1)}), bf16[8,32,2048]{2,1,0:T(8,128)(2,1)}, u32[]{:S(2)}, u32[]{:S(2)}) %all-to-all-start) | async-done | bytes 1048608 | tf_op jit(solution)/shard_map/all_to_all | solution.py:68
  230.8 3.0 fusion.10
  233.8 0.0 all-reduce.3.cloned.1.call-update
  233.8 0.2 reduce-scatter.5.cloned.1.call-start
  234.0 0.0 all-gather.5.cloned.1.call-done
  234.1 13.1 %convolution_convert_fusion.2 = bf16[512,2048]{1,0:T(8,128)(2,1)} fusion(bf16[512,3584]{1,0:T(8,128)(2,1)} %all-gather.5.cloned.1.call-done, bf16[3584,2048]{1,0:T(8,128)(2,1)} %param.12), kind=kOutput, calls=%fused_computation.5 | convolution fusion | flops 7517241344 | bytes 20447232 | tf_op jit(solution)/shard_map/dot_general | solution.py:41
  247.2 0.0 reduce-scatter.5.cloned.1.call-update
  247.2 16.4 %all-reduce.3.cloned.1.call-done = (bf16[4,8,8,128]{3,2,1,0:T(8,128)(2,1)}, bf16[4,8,8,128]{3,1,2,0:T(8,128)(2,1)}) async-done(((bf16[4,8,8,128]{3,2,1,0:T(8,128)(2,1)}, bf16[4,8,8,128]{3,1,2,0:T(8,128)(2,1)}), (bf16[4,8,8,128]{3,2,1,0:T(8,128)(2,1)}, bf16[4,8,8,128]{3,1,2,0:T(8,128)(2,1)})) %all-reduce.3.cloned.1.call-update) | async-done | bytes 131088 | tf_op jit(solution)/shard_map/psum | solution.py:74
  263.6 1.3 fusion
  264.9 1.1 copy.62
  266.0 5.5 %all-to-all-start.1 = ((bf16[8,32,2048]{2,1,0:T(8,128)(2,1)}), bf16[8,32,2048]{2,1,0:T(8,128)(2,1)}, u32[]{:S(2)}, u32[]{:S(2)}) async-start(bf16[8,32,2048]{2,1,0:T(8,128)(2,1)} %bitcast.75), calls=%async_computation.3 | async-start | bytes 2097152 | tf_op jit(solution)/shard_map/all_to_all | solution.py:86
  271.5 0.1 iota_compare_fusion.2
  271.7 2.1 bitcast_convert_fusion
  273.7 3.5 bitcast_convert_fusion.1
  277.2 36.2 %all-to-all-done.1 = bf16[8,32,2048]{2,1,0:T(8,128)(2,1)} async-done(((bf16[8,32,2048]{2,1,0:T(8,128)(2,1)}), bf16[8,32,2048]{2,1,0:T(8,128)(2,1)}, u32[]{:S(2)}, u32[]{:S(2)}) %all-to-all-start.1) | async-done | bytes 1048608 | tf_op jit(solution)/shard_map/all_to_all | solution.py:86
  313.4 1.5 fusion.23
  314.9 33.2 %reduce-scatter.5.cloned.1.call-done = bf16[64,2048]{1,0:T(8,128)(2,1)} async-done(((bf16[512,2048]{1,0:T(8,128)(2,1)}), bf16[64,2048]{1,0:T(8,128)(2,1)}) %reduce-scatter.5.cloned.1.call-update) | async-done | bytes 262160 | tf_op jit(solution)/shard_map/reduce_scatter | solution.py:40
  348.2 1.8 fusion.19
  (22 shorter events, 0.1 us)
Async XLA Ops:
  7.2 198.7 %copy-start = (bf16[4,128,2048]{2,1,0:T(8,128)(2,1)S(1)}, bf16[4,128,2048]{2,1,0:T(8,128)(2,1)}, u32[]{:S(2)}) copy-start(bf16[4,128,2048]{2,1,0:T(8,128)(2,1)} %param.14) | copy-start | bytes 6291460
  7.2 54.8 %all-gather.3.cloned.1.call-start = ((), (), s32[]{:S(2)}) async-start(), calls=%async_computation.5 | async-start | bytes 2359296 | tf_op jit(solution)/shard_map/all_gather | solution.py:32
  7.9 152.9 %reduce-scatter.3.cloned.1.call-start = ((), (), s32[]{:S(2)}) async-start(), calls=%async_computation.6 | async-start | bytes 9175040 | tf_op jit(solution)/shard_map/reduce_scatter | solution.py:36
  62.0 14.9 %copy-start.6 = (bf16[512,2048]{1,0:T(8,128)(2,1)S(1)}, bf16[512,2048]{1,0:T(8,128)(2,1)}, u32[]{:S(2)}) copy-start(bf16[512,2048]{1,0:T(8,128)(2,1)} %all-gather.3.cloned.1.call-done) | copy-start | bytes 6291460
  96.2 137.9 %all-gather.5.cloned.1.call-start = ((), (), s32[]{:S(2)}) async-start(), calls=%async_computation.7 | async-start | bytes 4587520 | tf_op jit(solution)/shard_map/all_gather | solution.py:39
  162.7 1.5 copy-start.4
  162.7 1.7 copy-start.3
  164.1 2.5 copy-start.5
  167.0 8.6 %copy-start.1 = (bf16[64,2048]{1,0:T(8,128)(2,1)S(1)}, bf16[64,2048]{1,0:T(8,128)(2,1)}, u32[]{:S(2)}) copy-start(bf16[64,2048]{1,0:T(8,128)(2,1)} %param.9) | copy-start | bytes 786436
  169.8 31.2 %all-to-all-start.2 = ((bf16[8,32,2048]{2,1,0:T(8,128)(2,1)}), bf16[8,32,2048]{2,1,0:T(8,128)(2,1)S(1)}, u32[]{:S(2)}, u32[]{:S(2)}) async-start(bf16[8,32,2048]{2,1,0:T(8,128)(2,1)} %bitcast.77), calls=%async_computation.4 | async-start | bytes 2097152 | tf_op jit(solution)/shard_map/all_to_all | solution.py:102
  201.0 29.8 %all-to-all-start = ((bf16[8,32,2048]{2,1,0:T(8,128)(2,1)}), bf16[8,32,2048]{2,1,0:T(8,128)(2,1)}, u32[]{:S(2)}, u32[]{:S(2)}) async-start(bf16[8,32,2048]{2,1,0:T(8,128)(2,1)} %bitcast.76), calls=%async_computation.2 | async-start | bytes 2097152 | tf_op jit(solution)/shard_map/all_to_all | solution.py:68
  205.2 58.4 %all-reduce.3.cloned.1.call-start = ((), (), s32[]{:S(2)}) async-start(), calls=%async_computation.9 | async-start | bytes 262144 | tf_op jit(solution)/shard_map/psum | solution.py:74
  233.8 114.4 %reduce-scatter.5.cloned.1.call-start = ((), (), s32[]{:S(2)}) async-start(), calls=%async_computation.8 | async-start | bytes 2359296 | tf_op jit(solution)/shard_map/reduce_scatter | solution.py:40
  264.9 6.7 %copy-start.2 = (bf16[4,8,8,128]{3,2,1,0:T(8,128)(2,1)S(1)}, bf16[4,8,8,128]{3,2,1,0:T(8,128)(2,1)}, u32[]{:S(2)}) copy-start(bf16[4,8,8,128]{3,2,1,0:T(8,128)(2,1)} %get-tuple-element.3) | copy-start | bytes 196612
  266.0 47.4 %all-to-all-start.1 = ((bf16[8,32,2048]{2,1,0:T(8,128)(2,1)}), bf16[8,32,2048]{2,1,0:T(8,128)(2,1)}, u32[]{:S(2)}, u32[]{:S(2)}) async-start(bf16[8,32,2048]{2,1,0:T(8,128)(2,1)} %bitcast.75), calls=%async_computation.3 | async-start | bytes 2097152 | tf_op jit(solution)/shard_map/all_to_all | solution.py:86
  271.5 2.2 copy-start.7
Sparse Core Ops, SparseCore 0:
  10.1 51.7 all-gather.2
  96.3 64.4 reduce-scatter.2
  164.3 31.4 all-gather.4
  233.9 29.6 all-reduce.2
  267.0 81.1 reduce-scatter.4
where the time goes:
time: 357 us
  waiting for transfers between devices  253 us (71%)
  matrix products  57.5 us (16%)
  starting transfers between devices  15.7 us (4%)
  between operations  14 us (4%)
  other arithmetic  12.2 us (3%)
  local copies, waits for them, and re-layouts  4.6 us (1%)
    reduce_scatter x1, waiting for transfers between devices, per_device(): lax.psum_scatter(partial_value.astype(jnp.bfloat16), 'tensor', scatter_di...  64.6 us
    all_gather x1, waiting for transfers between devices, per_device(): shard_rows = lax.all_gather(tokens, 'expert', axis=0, tiled=True)  54 us
    all_to_all x1, waiting for transfers between devices, per_device(): lax.all_to_all(expert_out.reshape(n_expert, per_peer, width_part), 'exper...  36.2 us
    reduce_scatter x1, waiting for transfers between devices, per_device(): lax.psum_scatter(jnp.dot(hidden_all, frozen_down_weight, preferred_elemen...  33.2 us
    all_to_all x1, waiting for transfers between devices, per_device(): lax.all_to_all(send_grads, 'expert', split_axis=0, concat_axis=0, tiled=T...  23.9 us
    all_to_all x1, waiting for transfers between devices, per_device(): lax.all_to_all(send_inputs, 'expert', split_axis=0, concat_axis=0, tiled=...  23.4 us
    psum x1, waiting for transfers between devices, per_device(): lax.psum(jnp.einsum('bcwk,cko->cbwo', incoming_input_rows, adapter_down_w...  16.4 us
    dot_general x1, matrix products, per_device(): jnp.dot(shard_rows, frozen_up_weight, preferred_element_type=jnp.float32)  14.9 us
  transfers between devices with their start and end apart: 8, of which 7 were waited for; matrix products, arithmetic and copies ran while one was open for 10% of the time, Pallas kernels for 0%

commit v1 on v0

v1 whole, which is shorter than its diff:
```python
import jax
import jax.numpy as jnp
from jax import lax
from jax.sharding import PartitionSpec as P

F32 = jnp.float32
BF16 = jnp.bfloat16


def activate(gate_part, up_part):
    return (jax.nn.silu(gate_part) * up_part).astype(BF16)


def frozen_layer(shard_rows, gate_weight, up_weight, down_weight):
    hidden_width = gate_weight.shape[1]
    gate_part = jnp.dot(shard_rows, gate_weight, preferred_element_type=F32).astype(BF16)
    up_part = jnp.dot(shard_rows, up_weight, preferred_element_type=F32).astype(BF16)
    summed = lax.psum_scatter(
        jnp.concatenate([gate_part, up_part], axis=1), "tensor", scatter_dimension=0, tiled=True
    ).astype(F32)
    hidden = activate(summed[:, :hidden_width], summed[:, hidden_width:])
    hidden_all = lax.all_gather(hidden, "tensor", axis=0, tiled=True)
    return jnp.dot(hidden_all, down_weight, preferred_element_type=F32)


def per_device(
    tokens,
    frozen_gate_weight,
    frozen_up_weight,
    frozen_down_weight,
    adapter_down_weight,
    adapter_up_weight,
    routes,
    route_gate_weights,
    output_gradient,
):
    n_expert = lax.axis_size("expert")
    tok_count, width_part = tokens.shape
    resident = adapter_down_weight.shape[0]
    most_slots = max(2, 4 * tok_count // (resident * n_expert))
    capacity = most_slots * n_expert
    total = tok_count * n_expert

    shard_rows = lax.all_gather(tokens, "expert", axis=0, tiled=True)
    meta = jnp.concatenate([routes.T.astype(F32), route_gate_weights.T], axis=0)
    meta_all = lax.all_gather(meta, "expert", axis=1, tiled=True)
    grad_rows = lax.all_gather(output_gradient, "expert", axis=0, tiled=True)

    local = (lax.axis_index("expert") * resident + jnp.arange(resident)).astype(F32)
    hit_0 = meta_all[0][None, :] == local[:, None]
    hit_1 = meta_all[1][None, :] == local[:, None]
    member = hit_0 | hit_1
    weight = jnp.where(hit_0, meta_all[2][None, :], 0.0) + jnp.where(
        hit_1, meta_all[3][None, :], 0.0
    )
    span = jnp.arange(tok_count)
    before = (span[:, None] < span[None, :]).astype(BF16)
    rank = jnp.dot(
        member.astype(BF16).reshape(resident * n_expert, tok_count),
        before,
        preferred_element_type=F32,
    ).reshape(resident, total)
    base_slot = (jnp.arange(total) // tok_count * most_slots).astype(F32)
    slot = jnp.where(member, rank + base_slot[None, :], -1.0)
    select = slot[:, None, :] == jnp.arange(capacity, dtype=F32)[None, :, None]
    slot_weight = jnp.sum(jnp.where(select, weight[:, None, :], 0.0), axis=2)
    pick = select.astype(BF16).reshape(resident * capacity, total)

    inputs = jnp.dot(pick, shard_rows, preferred_element_type=F32).astype(BF16)
    inputs = inputs.reshape(resident, capacity, width_part)
    cotangents = jnp.dot(pick, grad_rows, preferred_element_type=F32)
    scaled = (slot_weight[:, :, None] * cotangents.reshape(resident, capacity, width_part)).astype(
        BF16
    )
    low_part = jnp.einsum(
        "ecw,ewr->ecr", inputs, adapter_down_weight, preferred_element_type=F32
    ).astype(BF16)
    back_part = jnp.einsum(
        "ecw,erw->ecr", scaled, adapter_up_weight, preferred_element_type=F32
    ).astype(BF16)
    both = lax.psum(jnp.concatenate([low_part, back_part], axis=2), "tensor")
    rank_width = low_part.shape[2]
    low, back = both[:, :, :rank_width], both[:, :, rank_width:]
    grad_up = jnp.einsum("ecr,ecw->erw", low, scaled, preferred_element_type=F32).astype(BF16)
    grad_down = jnp.einsum("ecw,ecr->ewr", inputs, back, preferred_element_type=F32).astype(BF16)
    rows = jnp.einsum("ecr,erw->ecw", low, adapter_up_weight, preferred_element_type=F32)
    rows = (slot_weight[:, :, None] * rows).astype(BF16).reshape(resident * capacity, width_part)
    adapter_part = lax.dot_general(
        pick, rows, (((0,), (0,)), ((), ())), preferred_element_type=F32
    )

    base_part = frozen_layer(
        shard_rows, frozen_gate_weight, frozen_up_weight, frozen_down_weight
    )
    ffn_out = lax.psum_scatter(
        (base_part + adapter_part).astype(BF16), "expert", scatter_dimension=0, tiled=True
    )
    return (ffn_out, grad_down, grad_up)


def solution(mesh):
    placed = (
        P("expert", "tensor"),
        P("tensor", "expert"),
        P("tensor", "expert"),
        P("expert", "tensor"),
        P("expert", "tensor", None),
        P("expert", None, "tensor"),
        P("expert", None),
        P("expert", None),
        P("expert", "tensor"),
    )
    return jax.shard_map(
        per_device,
        mesh=mesh,
        in_specs=placed,
        out_specs=(P("expert", "tensor"), P("expert", "tensor", None), P("expert", None, "tensor")),
        check_vma=False,
    )
```

time: 357 us -> 359 us (level)
  blocking collectives: 0 us -> 26.2 us
  starting transfers between devices: 15.7 us -> 0.42 us
  waiting for transfers between devices: 253 us -> 248 us
    all_to_all x3 -> x0, waiting for transfers between devices: 83.5 us -> none  [the longest x1 36.2 us: per_device(): lax.all_to_all(expert_out.reshape(n_expert, per_peer, width_part), 'exper...]
    all_gather x1 -> x2, waiting for transfers between devices: 0.02 us -> 44.4 us  [the longest x1 26.3 us: frozen_layer(): hidden_all = lax.all_gather(hidden, 'tensor', axis=0, tiled=True)]
    reduce_scatter x2, waiting for transfers between devices: 97.8 us -> 127 us  [the longest x1 63.8 us: frozen_layer(): lax.psum_scatter(jnp.concatenate([gate_part, up_part], axis=1), 'tensor',...]
    all_gather x0 -> x1, blocking collectives: none -> 26.2 us  [per_device(): meta_all = lax.all_gather(meta, 'expert', axis=1, tiled=True)]
    all_to_all x3 -> x0, starting transfers between devices: 15.3 us -> none  [the longest x1 5.53 us: per_device(): lax.all_to_all(send_grads, 'expert', split_axis=0, concat_axis=0, tiled=T...]
    psum x1, waiting for transfers between devices: 16.4 us -> 21.1 us  [per_device(): both = lax.psum(jnp.concatenate([low_part, back_part], axis=2), 'tensor')]
    dot_general x12 -> x11, matrix products: 57.5 us -> 55.8 us  [the longest x1 14.9 us: frozen_layer(): jnp.dot(shard_rows, up_weight, preferred_element_type=F32).astype(BF16)]
    concatenate x1 -> x2, other arithmetic: 6.88 us -> 7.54 us  [the longest x1 6.87 us: frozen_layer(): jnp.concatenate([gate_part, up_part], axis=1)]
  transfers between devices with their start and end apart: 8 -> 6, of which waited for: 7 -> 6; matrix products, arithmetic and copies ran while one was open for 10% -> 8% of each run, Pallas kernels for 0% -> 0%
where the time goes in v1:
time: 359 us
  waiting for transfers between devices  248 us (69%)
  matrix products  55.8 us (16%)
  blocking collectives  26.2 us (7%)
  between operations  14.3 us (4%)
  other arithmetic  11.2 us (3%)
    reduce_scatter x1, waiting for transfers between devices, frozen_layer(): lax.psum_scatter(jnp.concatenate([gate_part, up_part], axis=1), 'tensor',...  63.8 us
    reduce_scatter x1, waiting for transfers between devices, per_device(): lax.psum_scatter((base_part + adapter_part).astype(BF16), 'expert', scatt...  63.4 us
    all_gather x1, waiting for transfers between devices, per_device(): shard_rows = lax.all_gather(tokens, 'expert', axis=0, tiled=True)  54 us
    all_gather x1, waiting for transfers between devices, frozen_layer(): hidden_all = lax.all_gather(hidden, 'tensor', axis=0, tiled=True)  26.3 us
    all_gather x1, blocking collectives, per_device(): meta_all = lax.all_gather(meta, 'expert', axis=1, tiled=True)  26.2 us
    psum x1, waiting for transfers between devices, per_device(): both = lax.psum(jnp.concatenate([low_part, back_part], axis=2), 'tensor')  21.1 us
    all_gather x1, waiting for transfers between devices, per_device(): grad_rows = lax.all_gather(output_gradient, 'expert', axis=0, tiled=True)  18.2 us
    dot_general x1, matrix products, frozen_layer(): jnp.dot(shard_rows, up_weight, preferred_element_type=F32).astype(BF16)  14.9 us
  transfers between devices with their start and end apart: 6, of which 6 were waited for; matrix products, arithmetic and copies ran while one was open for 8% of the time, Pallas kernels for 0%

profile of v1, /device:TPU:0, one launch (start us, length us, event | category | flops | bytes accessed | tf_op | source)
XLA Modules:
  0.0 358.7 jit_solution(514019846233866210)
XLA Ops:
  7.2 0.0 copy-start
  7.2 0.0 all-gather.5.cloned.1.call-start
  7.2 0.7 all-gather.5.cloned.1.call-update
  7.9 0.0 reduce-scatter.3.cloned.1.call-start
  8.0 54.0 %all-gather.5.cloned.1.call-done = bf16[512,2048]{1,0:T(8,128)(2,1)} async-done(((bf16[64,2048]{1,0:T(8,128)(2,1)}), bf16[512,2048]{1,0:T(8,128)(2,1)}) %all-gather.5.cloned.1.call-update) | async-done | bytes 2097168 | tf_op jit(solution)/shard_map/all_gather | solution.py:44
  62.0 14.9 %convolution_convert_fusion = bf16[512,3584]{1,0:T(8,128)(2,1)} fusion(bf16[512,2048]{1,0:T(8,128)(2,1)} %all-gather.5.cloned.1.call-done, bf16[2048,3584]{1,0:T(8,128)(2,1)} %param.11), kind=kOutput, calls=%fused_computation.1 | convolution fusion | flops 7518027776 | bytes 20447232 | tf_op jit(solution)/shard_map/dot_general | solution.py:17
  76.9 12.4 %convolution_convert_fusion.1 = bf16[512,3584]{1,0:T(8,128)(2,1)} fusion(bf16[512,2048]{1,0:T(8,128)(2,1)S(1)} %copy-done.4, bf16[2048,3584]{1,0:T(8,128)(2,1)} %param.10), kind=kOutput, calls=%fused_computation.2 | convolution fusion | flops 7518027776 | bytes 20447232 | tf_op jit(solution)/shard_map/dot_general | solution.py:16
  89.3 6.9 %pad_maximum_fusion = bf16[512,7168]{1,0:T(8,128)(2,1)} fusion(bf16[512,3584]{1,0:T(8,128)(2,1)} %convolution_convert_fusion, bf16[512,3584]{1,0:T(8,128)(2,1)} %convolution_convert_fusion.1), kind=kLoop, calls=%fused_computation | loop fusion | flops 14680064 | bytes 14680064 | tf_op jit(solution)/shard_map/concatenate | solution.py:19
  96.1 0.0 reduce-scatter.3.cloned.1.call-update
  96.2 0.0 all-gather.9.cloned.1.call-start
  96.2 0.7 all-gather.9.cloned.1.call-update
  96.9 0.0 all-gather.7.cloned.1.call-start
  96.9 63.8 %reduce-scatter.3.cloned.1.call-done = bf16[128,7168]{1,0:T(8,128)(2,1)} async-done(((bf16[512,7168]{1,0:T(8,128)(2,1)}), bf16[128,7168]{1,0:T(8,128)(2,1)}) %reduce-scatter.3.cloned.1.call-update) | async-done | bytes 1835024 | tf_op jit(solution)/shard_map/reduce_scatter | solution.py:18
  160.8 1.9 convert_element_type.61
  162.7 0.0 copy-start.6
  162.7 1.4 fusion.4
  164.1 0.0 all-gather.7.cloned.1.call-update
  164.1 0.0 all-reduce.2.cloned.1.call-start
  164.2 26.2 %all-gather = f32[8,64,4]{1,2,0:T(4,128)S(1)} all-gather(f32[1,64,4]{1,2,0:T(4,128)S(1)} %maximum_bitcast_fusion), channel_id=1, replica_groups=mesh['expert'=8,'tensor'=4] {'expert'}, dimensions={0}, use_global_device_ids=true | all-gather | bytes 9216 | tf_op jit(solution)/shard_map/all_gather | solution.py:46
  190.4 0.1 reshape.195
  190.5 0.1 eq.105
  190.6 0.1 eq.101
  190.7 0.1 eq.102
  190.8 0.1 eq.98
  190.9 0.2 fusion.12
  191.1 0.1 reshape.192
  191.1 0.1 eq.114
  191.2 0.1 add_select_fusion
  191.3 0.1 bitcast_compare_fusion
  191.5 0.1 select_reduce_fusion
  191.6 2.3 convolution_convert_fusion.4
  193.9 18.2 %all-gather.9.cloned.1.call-done = bf16[512,2048]{1,0:T(8,128)(2,1)} async-done(((bf16[64,2048]{1,0:T(8,128)(2,1)}), bf16[512,2048]{1,0:T(8,128)(2,1)}) %all-gather.9.cloned.1.call-update) | async-done | bytes 2097168 | tf_op jit(solution)/shard_map/all_gather | solution.py:47
  212.1 2.3 fusion.1
  214.4 0.8 convolution_convert_fusion.5
  215.3 1.1 copy-done.3
  216.4 0.5 convolution_convert_fusion.6
  216.9 0.7 pad_maximum_fusion.1
  217.6 0.0 all-reduce.2.cloned.1.call-update
  217.6 0.2 reduce-scatter.5.cloned.1.call-start
  217.9 26.3 %all-gather.7.cloned.1.call-done = bf16[512,3584]{1,0:T(8,128)(2,1)} async-done(((bf16[128,3584]{1,0:T(8,128)(2,1)}), bf16[512,3584]{1,0:T(8,128)(2,1)}) %all-gather.7.cloned.1.call-update) | async-done | bytes 3670032 | tf_op jit(solution)/shard_map/all_gather | solution.py:22
  244.1 13.5 %fusion.24 = f32[512,2048]{1,0:T(8,128)} fusion(bf16[512,3584]{1,0:T(8,128)(2,1)} %all-gather.7.cloned.1.call-done, bf16[3584,2048]{1,0:T(8,128)(2,1)} %param.12), kind=kOutput, calls=%fused_computation.54 | convolution fusion | flops 7516192768 | bytes 22544384 | tf_op jit(solution)/shard_map/dot_general | solution.py:23
  257.6 21.1 %all-reduce.2.cloned.1.call-done = bf16[4,64,256]{2,1,0:T(8,128)(2,1)} async-done(((bf16[4,64,256]{2,1,0:T(8,128)(2,1)}), bf16[4,64,256]{2,1,0:T(8,128)(2,1)}) %all-reduce.2.cloned.1.call-update) | async-done | bytes 131088 | tf_op jit(solution)/shard_map/psum | solution.py:81
  278.7 4.6 %fusion = bf16[512,2048]{1,0:T(8,128)(2,1)} fusion(f32[512,2048]{1,0:T(8,128)} %fusion.24, bf16[4,128,2048]{2,1,0:T(8,128)(2,1)S(1)} %copy-done, f32[4,64]{1,0:T(4,128)S(1)} %select_reduce_fusion, f32[4,512]{1,0:T(4,128)S(1)} %get-tuple-element.9, bf16[4,64,256]{2,1,0:T(8,128)(2,1)} %all-reduce.2.cloned.1.call-done), kind=kOutput, calls=%fused_computation.4 | convolution fusion | flops 674365440 | bytes 8463360 | tf_op jit(solution)/shard_map/dot_general | solution.py:88
  283.3 0.0 reduce-scatter.5.cloned.1.call-update
  283.3 0.9 copy-done.5
  284.2 2.2 convolution_convert_fusion.3
  286.4 2.1 convolution_convert_fusion.2
  288.5 63.4 %reduce-scatter.5.cloned.1.call-done = bf16[64,2048]{1,0:T(8,128)(2,1)} async-done(((bf16[512,2048]{1,0:T(8,128)(2,1)}), bf16[64,2048]{1,0:T(8,128)(2,1)}) %reduce-scatter.5.cloned.1.call-update) | async-done | bytes 262160 | tf_op jit(solution)/shard_map/reduce_scatter | solution.py:95
  (19 shorter events, 0.1 us)
Async XLA Ops:
  7.2 207.2 %copy-start = (bf16[4,128,2048]{2,1,0:T(8,128)(2,1)S(1)}, bf16[4,128,2048]{2,1,0:T(8,128)(2,1)}, u32[]{:S(2)}) copy-start(bf16[4,128,2048]{2,1,0:T(8,128)(2,1)} %param.14) | copy-start | bytes 6291460
  7.2 54.8 %all-gather.5.cloned.1.call-start = ((), (), s32[]{:S(2)}) async-start(), calls=%async_computation.2 | async-start | bytes 2359296 | tf_op jit(solution)/shard_map/all_gather | solution.py:44
  7.9 152.9 %reduce-scatter.3.cloned.1.call-start = ((), (), s32[]{:S(2)}) async-start(), calls=%async_computation.3 | async-start | bytes 9175040 | tf_op jit(solution)/shard_map/reduce_scatter | solution.py:18
  62.0 15.0 %copy-start.4 = (bf16[512,2048]{1,0:T(8,128)(2,1)S(1)}, bf16[512,2048]{1,0:T(8,128)(2,1)}, u32[]{:S(2)}) copy-start(bf16[512,2048]{1,0:T(8,128)(2,1)} %all-gather.5.cloned.1.call-done) | copy-start | bytes 6291460
  96.2 115.9 %all-gather.9.cloned.1.call-start = ((), (), s32[]{:S(2)}) async-start(), calls=%async_computation.5 | async-start | bytes 2359296 | tf_op jit(solution)/shard_map/all_gather | solution.py:47
  96.9 147.2 %all-gather.7.cloned.1.call-start = ((), (), s32[]{:S(2)}) async-start(), calls=%async_computation.4 | async-start | bytes 4587520 | tf_op jit(solution)/shard_map/all_gather | solution.py:22
  162.7 1.5 copy-start.6
  162.7 1.5 copy-start.7
  164.1 114.5 %all-reduce.2.cloned.1.call-start = ((), (), s32[]{:S(2)}) async-start(), calls=%async_computation.6 | async-start | bytes 262144 | tf_op jit(solution)/shard_map/psum | solution.py:81
  214.4 2.5 copy-start.1
  214.4 2.0 copy-start.3
  217.6 134.2 %reduce-scatter.5.cloned.1.call-start = ((), (), s32[]{:S(2)}) async-start(), calls=%async_computation.7 | async-start | bytes 2359296 | tf_op jit(solution)/shard_map/reduce_scatter | solution.py:95
  283.3 0.9 copy-start.5
  284.2 2.2 copy-start.2
Sparse Core Ops, SparseCore 0:
  10.1 51.7 all-gather.4
  96.3 64.4 reduce-scatter.2
  162.9 49.1 all-gather.8
  214.1 30.0 all-gather.6
  246.9 31.7 all-reduce.1
  283.4 68.3 reduce-scatter.4

commit v2 on v1

--- a/solution.py
+++ b/solution.py
@@ -1,6 +1,10 @@
+import functools
+
 import jax
 import jax.numpy as jnp
 from jax import lax
+from jax.experimental import pallas as pl
+from jax.experimental.pallas import tpu as pltpu
 from jax.sharding import PartitionSpec as P
 
 F32 = jnp.float32
@@ -11,13 +15,153 @@
     return (jax.nn.silu(gate_part) * up_part).astype(BF16)
 
 
-def frozen_layer(shard_rows, gate_weight, up_weight, down_weight):
-    hidden_width = gate_weight.shape[1]
+def place():
+    me = lax.axis_index("expert")
+    z, x = me // 2, me % 2
+    return me, z, x, z * 2 + 1 - x, [lax.rem(z + k, 4) for k in range(4)]
+
+
+def send(src, dst, send_sem, recv_sem, peer):
+    return pltpu.make_async_remote_copy(
+        src_ref=src, dst_ref=dst, send_sem=send_sem, recv_sem=recv_sem,
+        device_id={"expert": peer}, device_id_type=pl.DeviceIdType.MESH,
+    )
+
+
+def greet(x, partner, ahead):
+    barrier = pltpu.get_barrier_semaphore()
+    for peer in [partner] + [ahead[k] * 2 + x for k in (1, 2, 3)]:
+        pl.semaphore_signal(
+            barrier, inc=1, device_id={"expert": peer}, device_id_type=pl.DeviceIdType.MESH
+        )
+    pl.semaphore_wait(barrier, 4)
+
+
+def block(ref, index, rows):
+    return ref.at[pl.ds(pl.multiple_of(index * rows, rows), rows)]
+
+
+def gather_kernel(count, *refs):
+    sources, outs = refs[:count], refs[count:2 * count]
+    own_sem, z_send, z_recv, x_send, x_recv = refs[2 * count:]
+    me, z, x, partner, ahead = place()
+    greet(x, partner, ahead)
+    owns, sent = [], []
+    for a in range(count):
+        rows = sources[a].shape[0]
+        own = pltpu.make_async_copy(sources[a], block(outs[a], me, rows), own_sem.at[a])
+        own.start()
+        owns.append(own)
+        for k in (1, 2, 3):
+            i = 4 * a + k
+            copy = send(sources[a], block(outs[a], me, rows), z_send.at[i], z_recv.at[i],
+                        ahead[k] * 2 + x)
+            copy.start()
+            sent.append(copy)
+        copy = send(sources[a], block(outs[a], me, rows), x_send.at[4 * a], x_recv.at[4 * a],
+                    partner)
+        copy.start()
+        sent.append(copy)
+    for k in (1, 2, 3):
+        origin = ahead[4 - k] * 2
+        for a in range(count):
+            rows = sources[a].shape[0]
+            i = 4 * a + k
+            landed = block(outs[a], origin + x, rows)
+            send(sources[a], landed, z_send.at[i], z_recv.at[i], partner).wait_recv()
+            copy = send(landed, landed, x_send.at[i], x_recv.at[i], partner)
+            copy.start()
+            sent.append(copy)
+    for k in range(4):
+        origin = ahead[(4 - k) % 4] * 2 + 1 - x
+        for a in range(count):
+            rows = sources[a].shape[0]
+            i = 4 * a + k
+            send(sources[a], block(outs[a], origin, rows), x_send.at[i], x_recv.at[i],
+                 partner).wait_recv()
+    for copy in sent:
+        copy.wait_send()
+    for own in owns:
+        own.wait()
+
+
+def gather_rows(arrays, collective):
+    count = len(arrays)
+    vmem = pl.BlockSpec(memory_space=pltpu.VMEM)
+    return pl.pallas_call(
+        functools.partial(gather_kernel, count),
+        out_shape=[jax.ShapeDtypeStruct((8 * a.shape[0], a.shape[1]), a.dtype) for a in arrays],
+        in_specs=[vmem] * count,
+        out_specs=[vmem] * count,
+        scratch_shapes=[pltpu.SemaphoreType.DMA((count,))]
+        + [pltpu.SemaphoreType.DMA((4 * count,))] * 4,
+        compiler_params=pltpu.CompilerParams(
+            collective_id=collective, has_side_effects=True, vmem_limit_bytes=16 << 20
+        ),
+    )(*arrays)
+
+
+def scatter_kernel(part, out, x_buf, sums, z_buf, x_send, x_recv, z_send, z_recv):
+    me, z, x, partner, ahead = place()
+    rows = out.shape[0]
+    greet(x, partner, ahead)
+    across, along = {}, []
+    for k in (2, 1, 3, 0):
+        across[k] = send(block(part, ahead[k] * 2 + 1 - x, rows), x_buf.at[k], x_send.at[k],
+                         x_recv.at[k], partner)
+        across[k].start()
+    for k in (2, 1, 3):
+        across[k].wait_recv()
+        mine = part[pl.ds(pl.multiple_of((ahead[k] * 2 + x) * rows, rows), rows), :]
+        sums[k - 1] = (mine.astype(F32) + x_buf[k].astype(F32)).astype(BF16)
+        copy = send(sums.at[k - 1], z_buf.at[k - 1], z_send.at[k - 1], z_recv.at[k - 1],
+                    ahead[k] * 2 + x)
+        copy.start()
+        along.append(copy)
+    across[0].wait_recv()
+    for copy in along:
+        copy.wait_recv()
+    mine = part[pl.ds(pl.multiple_of(me * rows, rows), rows), :]
+    total = mine.astype(F32) + x_buf[0].astype(F32)
+    for k in range(3):
+        total += z_buf[k].astype(F32)
+    out[...] = total.astype(BF16)
+    for k in range(4):
+        across[k].wait_send()
+    for copy in along:
+        copy.wait_send()
+
+
+def scatter_rows(part, collective):
+    rows, width = part.shape[0] // 8, part.shape[1]
+    vmem = pl.BlockSpec(memory_space=pltpu.VMEM)
+    return pl.pallas_call(
+        scatter_kernel,
+        out_shape=jax.ShapeDtypeStruct((rows, width), BF16),
+        in_specs=[vmem],
+        out_specs=vmem,
+        scratch_shapes=[
+            pltpu.VMEM((4, rows, width), BF16),
+            pltpu.VMEM((3, rows, width), BF16),
+            pltpu.VMEM((3, rows, width), BF16),
+        ]
+        + [pltpu.SemaphoreType.DMA((4,))] * 2
+        + [pltpu.SemaphoreType.DMA((3,))] * 2,
+        compiler_params=pltpu.CompilerParams(
+            collective_id=collective, has_side_effects=True, vmem_limit_bytes=16 << 20
+        ),
+    )(part)
+
+
+def gate_up_part(shard_rows, gate_weight, up_weight):
     gate_part = jnp.dot(shard_rows, gate_weight, preferred_element_type=F32).astype(BF16)
     up_part = jnp.dot(shard_rows, up_weight, preferred_element_type=F32).astype(BF16)
-    summed = lax.psum_scatter(
-        jnp.concatenate([gate_part, up_part], axis=1), "tensor", scatter_dimension=0, tiled=True
-    ).astype(F32)
+    return jnp.concatenate([gate_part, up_part], axis=1)
+
+
+def down_part(summed, down_weight):
+    hidden_width = down_weight.shape[0]
+    summed = summed.astype(F32)
     hidden = activate(summed[:, :hidden_width], summed[:, hidden_width:])
     hidden_all = lax.all_gather(hidden, "tensor", axis=0, tiled=True)
     return jnp.dot(hidden_all, down_weight, preferred_element_type=F32)
@@ -41,10 +185,27 @@
     capacity = most_slots * n_expert
     total = tok_count * n_expert
 
-    shard_rows = lax.all_gather(tokens, "expert", axis=0, tiled=True)
+    direct = n_expert == 8 and lax.axis_size("tensor") == 4
     meta = jnp.concatenate([routes.T.astype(F32), route_gate_weights.T], axis=0)
-    meta_all = lax.all_gather(meta, "expert", axis=1, tiled=True)
-    grad_rows = lax.all_gather(output_gradient, "expert", axis=0, tiled=True)
+    if direct:
+        shard_rows = gather_rows([tokens], 0)[0]
+    else:
+        shard_rows = lax.all_gather(tokens, "expert", axis=0, tiled=True)
+    gate_up = gate_up_part(shard_rows, frozen_gate_weight, frozen_up_weight)
+    if direct:
+        meta_pad = jnp.pad(meta, ((0, 4), (0, 128 - tok_count)))
+        gate_up, output_gradient, meta_pad = lax.optimization_barrier(
+            (gate_up, output_gradient, meta_pad)
+        )
+        summed = lax.psum_scatter(gate_up, "tensor", scatter_dimension=0, tiled=True)
+        grad_rows, meta_rows = gather_rows([output_gradient, meta_pad], 1)
+        summed, grad_rows, meta_rows = lax.optimization_barrier((summed, grad_rows, meta_rows))
+        meta_all = meta_rows.reshape(8, 8, 128)[:, :4, :tok_count].transpose(1, 0, 2)
+        meta_all = meta_all.reshape(4, total)
+    else:
+        summed = lax.psum_scatter(gate_up, "tensor", scatter_dimension=0, tiled=True)
+        meta_all = lax.all_gather(meta, "expert", axis=1, tiled=True)
+        grad_rows = lax.all_gather(output_gradient, "expert", axis=0, tiled=True)
 
     local = (lax.axis_index("expert") * resident + jnp.arange(resident)).astype(F32)
     hit_0 = meta_all[0][None, :] == local[:, None]
@@ -89,12 +250,11 @@
         pick, rows, (((0,), (0,)), ((), ())), preferred_element_type=F32
     )
 
-    base_part = frozen_layer(
-        shard_rows, frozen_gate_weight, frozen_up_weight, frozen_down_weight
-    )
-    ffn_out = lax.psum_scatter(
-        (base_part + adapter_part).astype(BF16), "expert", scatter_dimension=0, tiled=True
-    )
+    part = (down_part(summed, frozen_down_weight) + adapter_part).astype(BF16)
+    if direct:
+        ffn_out = scatter_rows(part, 2)
+    else:
+        ffn_out = lax.psum_scatter(part, "expert", scatter_dimension=0, tiled=True)
     return (ffn_out, grad_down, grad_up)
 
 

time: 359 us -> 279 us (0.78)
  waiting for transfers between devices: 248 us -> 87.8 us
  Pallas kernels: 0 us -> 107 us
  blocking collectives: 26.2 us -> 0 us
  local copies, waits for them, and re-layouts: 2.63 us -> 7.92 us
  matrix products: 55.8 us -> 50.7 us
    pallas_call x0 -> x3, Pallas kernels: none -> 107 us  [the longest x2 72.4 us: gather_rows(): pl.pallas_call(functools.partial(gather_kernel, count), out_shape=[jax.Sh...]
    reduce_scatter x2 -> x1, waiting for transfers between devices: 127 us -> 31.8 us  [per_device(): lax.psum_scatter(gate_up, 'tensor', scatter_dimension=0, tiled=True)]
    all_gather x3 -> x1, waiting for transfers between devices: 98.4 us -> 27.5 us  [down_part(): hidden_all = lax.all_gather(hidden, 'tensor', axis=0, tiled=True)]
    all_gather x1 -> x0, blocking collectives: 26.2 us -> none  [per_device(): meta_all = lax.all_gather(meta, 'expert', axis=1, tiled=True)]
    psum x1, waiting for transfers between devices: 21.1 us -> 28.4 us  [per_device(): both = lax.psum(jnp.concatenate([low_part, back_part], axis=2), 'tensor')]
    unnamed x17 -> x33, local copies, waits for them, and re-layouts: 2.12 us -> 7.23 us
    dot_general x3, matrix products: 40.8 us -> 35.8 us  [the longest x1 13.4 us: down_part(): return jnp.dot(hidden_all, down_weight, preferred_element_type=F32)]
  transfers between devices with their start and end apart: 6 -> 3, of which waited for: 6 -> 3; matrix products, arithmetic and copies ran while one was open for 8% -> 3% of each run, Pallas kernels for 0% -> 13%
where the time goes in v2:
time: 279 us
  Pallas kernels  107 us (38%)
  waiting for transfers between devices  87.8 us (31%)
  matrix products  50.7 us (18%)
  between operations  14 us (5%)
  other arithmetic  11.2 us (4%)
  local copies, waits for them, and re-layouts  7.92 us (3%)
    pallas_call x2, Pallas kernels, gather_rows(): pl.pallas_call(functools.partial(gather_kernel, count), out_shape=[jax.Sh...  72.4 us
    pallas_call x1, Pallas kernels, scatter_rows(): pl.pallas_call(scatter_kernel, out_shape=jax.ShapeDtypeStruct((rows, widt...  34.8 us
    reduce_scatter x1, waiting for transfers between devices, per_device(): lax.psum_scatter(gate_up, 'tensor', scatter_dimension=0, tiled=True)  31.8 us
    psum x1, waiting for transfers between devices, per_device(): both = lax.psum(jnp.concatenate([low_part, back_part], axis=2), 'tensor')  28.4 us
    all_gather x1, waiting for transfers between devices, down_part(): hidden_all = lax.all_gather(hidden, 'tensor', axis=0, tiled=True)  27.5 us
    dot_general x1, matrix products, down_part(): return jnp.dot(hidden_all, down_weight, preferred_element_type=F32)  13.4 us
    dot_general x1, matrix products, gate_up_part(): jnp.dot(shard_rows, up_weight, preferred_element_type=F32).astype(BF16)  13.2 us
    dot_general x1, matrix products, gate_up_part(): jnp.dot(shard_rows, gate_weight, preferred_element_type=F32).astype(BF16)  9.29 us
  transfers between devices with their start and end apart: 3, of which 3 were waited for; matrix products, arithmetic and copies ran while one was open for 3% of the time, Pallas kernels for 13%

profile of v2, /device:TPU:0, one launch (start us, length us, event | category | flops | bytes accessed | tf_op | source)
XLA Modules:
  0.0 279.2 jit_solution(9233712308051842241)
XLA Ops:
  7.2 0.0 copy-start
  7.2 0.0 reduce-scatter.2.cloned.1.call-start
  7.2 1.1 copy-done.3
  8.3 36.7 %shard_map.112 = bf16[512,2048]{1,0:T(8,128)(2,1)S(1)} custom-call(bf16[64,2048]{1,0:T(8,128)(2,1)S(1)} %copy-done.3), custom_call_target="tpu_custom_call" | custom-call | tf_op jit(solution)/shard_map/pallas_call | solution.py:91
  45.0 0.0 slice-start.1
  45.1 13.2 %convolution_convert_fusion = bf16[512,3584]{1,0:T(8,128)(2,1)} fusion(bf16[512,2048]{1,0:T(8,128)(2,1)S(1)} %shard_map.112, bf16[2048,3584]{1,0:T(8,128)(2,1)} %param.11), kind=kOutput, calls=%fused_computation.1 | convolution fusion | flops 7518027776 | bytes 20447232 | tf_op jit(solution)/shard_map/dot_general | solution.py:158
  58.3 9.3 %convolution_convert_fusion.1 = bf16[512,3584]{1,0:T(8,128)(2,1)} fusion(bf16[512,2048]{1,0:T(8,128)(2,1)S(1)} %shard_map.112, bf16[2048,3584]{1,0:T(8,128)(2,1)S(1)} %bitcast.50), kind=kOutput, calls=%fused_computation.2 | convolution fusion | flops 7518027776 | bytes 20447232 | tf_op jit(solution)/shard_map/dot_general | solution.py:157
  67.6 6.9 %pad_maximum_fusion = bf16[512,7168]{1,0:T(8,128)(2,1)} fusion(bf16[512,3584]{1,0:T(8,128)(2,1)} %convolution_convert_fusion, bf16[512,3584]{1,0:T(8,128)(2,1)} %convolution_convert_fusion.1), kind=kLoop, calls=%fused_computation | loop fusion | flops 14680064 | bytes 14680064 | tf_op jit(solution)/shard_map/concatenate | solution.py:159
  74.5 0.0 reduce-scatter.2.cloned.1.call-update
  74.5 0.0 all-reduce.3.cloned.1.call-start
  74.6 0.1 eq.101
  74.6 0.1 eq.102
  74.7 0.1 eq.114
  74.8 0.6 copy-done.4
  75.4 35.7 %shard_map.113 = (bf16[512,2048]{1,0:T(8,128)(2,1)S(1)}, f32[64,128]{1,0:T(8,128)S(1)}) custom-call(bf16[64,2048]{1,0:T(8,128)(2,1)S(1)} %copy-done.4, f32[8,128]{1,0:T(8,128)S(1)} %select_maximum_fusion.refs_1_), custom_call_target="tpu_custom_call" | custom-call | tf_op jit(solution)/shard_map/pallas_call | solution.py:91
  111.2 1.3 copy-done.5
  112.5 31.8 %reduce-scatter.2.cloned.1.call-done = bf16[128,7168]{1,0:T(8,128)(2,1)} async-done(((bf16[512,7168]{1,0:T(8,128)(2,1)}), bf16[128,7168]{1,0:T(8,128)(2,1)}) %reduce-scatter.2.cloned.1.call-update) | async-done | bytes 1835024 | tf_op jit(solution)/shard_map/reduce_scatter | solution.py:200
  144.3 0.1 slice_reduce_fusion.3
  144.4 0.2 fusion.12
  144.6 0.1 reshape.211
  144.6 0.1 broadcast_in_dim.49
  144.7 0.1 broadcast_in_dim.52
  144.8 0.1 eq.91
  144.9 0.1 eq.95
  144.9 0.1 add_select_fusion
  145.0 0.1 bitcast_compare_fusion
  145.2 2.4 convolution_convert_fusion.4
  147.6 0.1 select_reduce_fusion
  147.8 0.5 convolution_convert_fusion.6
  148.3 0.9 copy-done.6
  149.2 0.7 fusion.1
  150.0 1.0 copy-done.7
  150.9 0.8 convolution_convert_fusion.5
  151.8 0.7 pad_maximum_fusion.1
  152.4 0.0 all-reduce.3.cloned.1.call-update
  152.5 0.2 all-gather.2.cloned.1.call-start
  152.7 1.9 convert_element_type.65
  154.6 1.4 fusion.4
  156.0 0.0 all-gather.2.cloned.1.call-update
  156.0 28.4 %all-reduce.3.cloned.1.call-done = bf16[4,64,256]{2,1,0:T(8,128)(2,1)} async-done(((bf16[4,64,256]{2,1,0:T(8,128)(2,1)}), bf16[4,64,256]{2,1,0:T(8,128)(2,1)}) %all-reduce.3.cloned.1.call-update) | async-done | bytes 131088 | tf_op jit(solution)/shard_map/psum | solution.py:242
  184.4 3.4 %convolution_convert_fusion.2 = bf16[4,128,2048]{2,1,0:T(8,128)(2,1)} fusion(bf16[4,64,2048]{2,1,0:T(8,128)(2,1)} %copy-done.7, bf16[4,64,256]{2,1,0:T(8,128)(2,1)} %all-reduce.3.cloned.1.call-done), kind=kOutput, calls=%fused_computation.5 | convolution fusion | flops 135266304 | bytes 3211264 | tf_op jit(solution)/shard_map/ecr,ecw->erw/dot_general | solution.py:245
  187.8 2.2 convolution_convert_fusion.3
  190.0 27.5 %all-gather.2.cloned.1.call-done = bf16[512,3584]{1,0:T(8,128)(2,1)} async-done(((bf16[128,3584]{1,0:T(8,128)(2,1)}), bf16[512,3584]{1,0:T(8,128)(2,1)}) %all-gather.2.cloned.1.call-update) | async-done | bytes 3670032 | tf_op jit(solution)/shard_map/all_gather | solution.py:166
  217.5 13.4 %fusion.24 = f32[512,2048]{1,0:T(8,128)} fusion(bf16[512,3584]{1,0:T(8,128)(2,1)} %all-gather.2.cloned.1.call-done, bf16[3584,2048]{1,0:T(8,128)(2,1)} %param.12), kind=kOutput, calls=%fused_computation.59 | convolution fusion | flops 7516192768 | bytes 22544384 | tf_op jit(solution)/shard_map/dot_general | solution.py:167
  230.9 4.6 %fusion.part = bf16[512,2048]{1,0:T(8,128)(2,1)} fusion(f32[512,2048]{1,0:T(8,128)} %fusion.24, bf16[4,128,2048]{2,1,0:T(8,128)(2,1)S(1)} %copy-done, f32[4,64]{1,0:T(4,128)S(1)} %select_reduce_fusion, f32[4,512]{1,0:T(4,128)S(1)} %get-tuple-element.25, bf16[4,64,256]{2,1,0:T(8,128)(2,1)S(1)} %copy-done.9), kind=kOutput, calls=%fused_computation.4 | convolution fusion | flops 674365440 | bytes 8464384 | tf_op jit(solution)/shard_map/dot_general | solution.py:249
  235.5 1.6 copy-done.2
  237.1 34.8 %shard_map.114 = bf16[64,2048]{1,0:T(8,128)(2,1)S(1)} custom-call(bf16[512,2048]{1,0:T(8,128)(2,1)S(1)} %copy-done.2), custom_call_target="tpu_custom_call" | custom-call | tf_op jit(solution)/shard_map/pallas_call | solution.py:138
  271.9 0.7 copy.16
  (31 shorter events, 0.1 us)
Async XLA Ops:
  7.2 143.8 %copy-start = (bf16[4,128,2048]{2,1,0:T(8,128)(2,1)S(1)}, bf16[4,128,2048]{2,1,0:T(8,128)(2,1)}, u32[]{:S(2)}) copy-start(bf16[4,128,2048]{2,1,0:T(8,128)(2,1)} %param.14) | copy-start | bytes 6291460
  7.2 137.1 %reduce-scatter.2.cloned.1.call-start = ((), (), s32[]{:S(2)}) async-start(), calls=%async_computation.1 | async-start | bytes 9175040 | tf_op jit(solution)/shard_map/reduce_scatter | solution.py:200
  7.2 1.1 copy-start.3
  8.3 49.9 %slice-start = ((s8[14680064]{0:T(1024)(128)(4,1)}), s8[4194304]{0:T(1024)(128)(4,1)S(1)}, s32[]{:S(2)}) async-start(s8[14680064]{0:T(1024)(128)(4,1)} %bitcast.49), calls=%async_computation.4 | async-start | bytes 8388608
  45.0 13.2 %copy-start.1 = (bf16[512,2048]{1,0:T(8,128)(2,1)}, bf16[512,2048]{1,0:T(8,128)(2,1)S(1)}, u32[]{:S(2)}) copy-start(bf16[512,2048]{1,0:T(8,128)(2,1)S(1)} %shard_map.112) | copy-start | bytes 6291460
  45.0 13.2 %slice-start.1 = ((s8[14680064]{0:T(1024)(128)(4,1)}), s8[4194304]{0:T(1024)(128)(4,1)S(1)}, s32[]{:S(2)}) async-start(s8[14680064]{0:T(1024)(128)(4,1)} %bitcast.49), calls=%async_computation.5 | async-start | bytes 8388608
  45.0 13.2 %slice-start.2 = ((s8[14680064]{0:T(1024)(128)(4,1)}), s8[4194304]{0:T(1024)(128)(4,1)S(1)}, s32[]{:S(2)}) async-start(s8[14680064]{0:T(1024)(128)(4,1)} %bitcast.49), calls=%async_computation.6 | async-start | bytes 8388608
  45.0 13.2 %slice-start.3 = ((s8[14680064]{0:T(1024)(128)(4,1)}), s8[2097152]{0:T(1024)(128)(4,1)S(1)}, s32[]{:S(2)}) async-start(s8[14680064]{0:T(1024)(128)(4,1)} %bitcast.49), calls=%async_computation.7 | async-start | bytes 4194304
  58.3 9.3 %copy-start.10 = (s32[64,2]{0,1:T(2,128)S(1)}, s32[64,2]{0,1:T(2,128)}, u32[]{:S(2)}) copy-start(s32[64,2]{0,1:T(2,128)} %param.15) | copy-start | bytes 1540
  67.6 6.9 %copy-start.11 = (f32[64,2]{0,1:T(2,128)S(1)}, f32[64,2]{0,1:T(2,128)}, u32[]{:S(2)}) copy-start(f32[64,2]{0,1:T(2,128)} %param.16) | copy-start | bytes 1540
  74.5 1.0 copy-start.4
  74.5 109.9 %all-reduce.3.cloned.1.call-start = ((), (), s32[]{:S(2)}) async-start(), calls=%async_computation.3 | async-start | bytes 262144 | tf_op jit(solution)/shard_map/psum | solution.py:242
  111.2 1.3 copy-start.5
  144.9 2.8 %copy-start.8 = (bf16[4,2048,128]{2,1,0:T(8,128)(2,1)S(1)}, bf16[4,2048,128]{2,1,0:T(8,128)(2,1)}, u32[]{:S(2)}) copy-start(bf16[4,2048,128]{2,1,0:T(8,128)(2,1)} %param.13) | copy-start | bytes 6291460
  147.6 1.6 copy-start.6
  149.9 1.0 copy-start.7
  152.5 65.0 %all-gather.2.cloned.1.call-start = ((), (), s32[]{:S(2)}) async-start(), calls=%async_computation.2 | async-start | bytes 4587520 | tf_op jit(solution)/shard_map/all_gather | solution.py:166
  184.4 3.4 %copy-start.9 = (bf16[4,64,256]{2,1,0:T(8,128)(2,1)S(1)}, bf16[4,64,256]{2,1,0:T(8,128)(2,1)}, u32[]{:S(2)}) copy-start(bf16[4,64,256]{2,1,0:T(8,128)(2,1)} %all-reduce.3.cloned.1.call-done) | copy-start | bytes 393220
  235.5 1.6 copy-start.2
Sparse Core Ops, SparseCore 0:
  74.6 69.6 reduce-scatter.1
  152.6 31.7 all-reduce.2
  186.0 31.4 all-gather.1
